TPU v7x, 256 devices: a whole 4x4x8 slice. The times are simulated.
256 devices in a mesh: rows: 8 (over y, core), labels: 32 (over x, z).
Axes of the slice: x: 4, y: 4, z: 8, core: 2. Of those that a mesh axis runs over, the one named last changes fastest.
Arguments:
- embeddings: bfloat16 [8192, 768], P(('rows', 'labels')), may hold values from -6 to 6
- class_weight: bfloat16 [65536, 768], P('labels'), may hold values from -0.4375 to 0.4375
- class_bias: float32 [65536], P('labels'), may hold values from -10 to -8
- propensity: float32 [65536], P('labels'), may hold values from 0.1 to 0.9
- label_ids: int32 [8192, 32], P('rows'), may hold values from 0 to 65535
- label_count: int32 [8192], P('rows'), may hold values from 1 to 32
- label_bins: int32 [65536], P('labels'), may hold values from 0 to 15
- prior_mean: float32 [16], replicated, may hold values from 0.1 to 0.9
Outputs:
- new_propensity: float32 [65536], P('labels')
- weight_grad: bfloat16 [65536, 768], P('labels', 'rows')
- embed_grad: bfloat16 [8192, 768], P(('rows', 'labels'))
Inputs may be any that keep to these rules, and one draw needn't show every extreme that they name: `label_ids`: entries past a row's count are padding and are ignored; ids may repeat.
All inputs are finite; a program needn't handle non-finite values.
Results may differ from a plain program's by a relative error of at most 0.014.
Values may be sent and summed in bfloat16 or wider, within the bound.
No kernel may reach another device: no remote copies, remote signals or barrier semaphores. Data moves between devices by JAX's collectives and lax.ppermute only.
A program may use at most 64 MiB of HBM per device.

v0:
```python
import functools

import jax
import jax.numpy as jnp
from jax import lax
from jax.experimental import pallas as pl
from jax.experimental.pallas import tpu as pltpu
from jax.sharding import Mesh, PartitionSpec as P

BF = jnp.bfloat16
F32 = jnp.float32
LANES = 128
LOG2E = 1.4426950408889634
NX, NZ, NY, NC = 4, 8, 4, 2


def ring(n, d):
    return [(i, (i + d) % n) for i in range(n)]


def mm(a, b, dims):
    return lax.dot_general(a, b, (dims, ((), ())), preferred_element_type=F32)


def observed_words(label_ids, label_count, offset, width):
    slots = jnp.arange(label_ids.shape[1], dtype=jnp.int32)
    local = label_ids - offset
    valid = (slots[None, :] < label_count[:, None]) & (local >= 0) & (local < width)
    lane = jnp.where(valid, local & (LANES - 1), -1)
    word = jnp.left_shift(jnp.int32(1), jnp.where(valid, local >> 7, 0))
    lanes = jnp.arange(LANES, dtype=jnp.int32)
    hits = jnp.where(lane[:, :, None] == lanes[None, None, :], word[:, :, None], 0)
    return lax.reduce(hits, jnp.int32(0), lax.bitwise_or, (1,))


def score_kernel(*refs, count, chunk, tile):
    x_refs, words_refs = refs[:count], refs[count : 2 * count]
    w_ref, bias_ref, prop_ref = refs[2 * count : 2 * count + 3]
    res_refs, post_ref = refs[2 * count + 3 : -1], refs[-1]
    step = pl.program_id(0)
    cols = pl.ds(pl.multiple_of(step * tile, tile), tile)
    lowest = step * (tile // LANES)
    bias = bias_ref[...] * -LOG2E
    prop = prop_ref[...]
    rest = 1.0 - prop
    total = jnp.zeros((8, tile), F32)
    for x_ref, words_ref, res_ref in zip(x_refs, words_refs, res_refs):
        size = min(chunk, x_ref.shape[0])
        for start in range(0, x_ref.shape[0], size):
            rows = slice(start, start + size)
            scores = mm(x_ref[rows, :], w_ref[cols, :], ((1,), (1,)))
            grown = 1.0 + jnp.exp2(scores * -LOG2E + bias)
            prob = 1.0 / grown
            unseen = rest / (grown - prop)
            words = words_ref[rows, :]
            seen = jnp.concatenate(
                [words & jnp.left_shift(jnp.int32(1), lowest + b) for b in range(tile // LANES)],
                axis=1,
            )
            posterior = jnp.where(seen != 0, 1.0, unseen)
            res_ref[rows, :] = (prob - posterior).astype(BF)
            total = total + jnp.sum(posterior.reshape(size // 8, 8, tile), axis=0)
    post_ref[...] = jnp.sum(total, axis=0, keepdims=True)


def in_vmem(count):
    return [pl.BlockSpec(memory_space=pltpu.VMEM)] * count


def score_call(xs, words, w, bias, prop, chunk=256, tile=512):
    width, depth = w.shape
    rows = sum(x.shape[0] for x in xs)
    narrow = pl.BlockSpec((1, tile), lambda i: (0, i))
    *res, post = pl.pallas_call(
        functools.partial(score_kernel, count=len(xs), chunk=chunk, tile=tile),
        grid=(width // tile,),
        in_specs=in_vmem(2 * len(xs) + 1) + [narrow, narrow],
        out_specs=[pl.BlockSpec((x.shape[0], tile), lambda i: (0, i)) for x in xs] + [narrow],
        out_shape=[pltpu.HBM((x.shape[0], width), BF) for x in xs]
        + [jax.ShapeDtypeStruct((1, width), F32)],
        cost_estimate=pl.CostEstimate(
            flops=2 * rows * width * depth,
            bytes_accessed=2 * (rows * depth + width * depth + rows * width),
            transcendentals=3 * rows * width,
        ),
        compiler_params=pltpu.CompilerParams(vmem_limit_bytes=24 << 20),
        name="scores",
    )(*xs, *words, w, bias, prop)
    return res, post


def weight_kernel(*refs, count):
    x_refs, r_refs = refs[:count], refs[count : 2 * count]
    out_ref, x_all, r_all = refs[2 * count :]

    @pl.when(pl.program_id(0) == 0)
    def _():
        at = 0
        for x_ref in x_refs:
            x_all[at : at + x_ref.shape[0], :] = x_ref[...]
            at += x_ref.shape[0]

    at = 0
    for r_ref in r_refs:
        r_all[at : at + r_ref.shape[0], :] = r_ref[...]
        at += r_ref.shape[0]
    out_ref[...] = mm(x_all[...], r_all[...], ((0,), (0,))).astype(BF)


def weight_call(xs, rs, tile=512):
    depth = xs[0].shape[1]
    width = rs[0].shape[1]
    rows = sum(x.shape[0] for x in xs)
    return pl.pallas_call(
        functools.partial(weight_kernel, count=len(xs)),
        grid=(width // tile,),
        in_specs=[pl.BlockSpec(x.shape, lambda i: (0, 0)) for x in xs]
        + [pl.BlockSpec((r.shape[0], tile), lambda i: (0, i)) for r in rs],
        out_specs=pl.BlockSpec((depth, tile), lambda i: (0, i)),
        out_shape=jax.ShapeDtypeStruct((depth, width), BF),
        scratch_shapes=[pltpu.VMEM((rows, depth), BF), pltpu.VMEM((rows, tile), BF)],
        cost_estimate=pl.CostEstimate(
            flops=2 * rows * width * depth,
            bytes_accessed=2 * (rows * (depth + width) + width * depth),
            transcendentals=0,
        ),
        compiler_params=pltpu.CompilerParams(vmem_limit_bytes=24 << 20),
        name="weights",
    )(*xs, *rs)


def sum_over_y(v):
    one, two, three = (lax.ppermute(v, "y", ring(NY, d)) for d in (1, 2, 3))
    return (v + two) + (one + three)


def pair_blocks(terms):
    core, y = lax.axis_index("core"), lax.axis_index("y")
    given = lax.dynamic_index_in_dim(terms, 1 - core, 1, keepdims=False)
    kept = lax.dynamic_index_in_dim(terms, core, 1, keepdims=False)
    pair = kept.astype(F32) + lax.ppermute(given, "core", ring(NC, 1)).astype(F32)
    pair = pair.astype(BF)
    return [lax.dynamic_index_in_dim(pair, (y + d) % NY, 0, keepdims=False) for d in range(NY)]


def bin_prior(bins, prior_mean):
    levels = jnp.arange(prior_mean.shape[0], dtype=jnp.int32)
    onehot = (bins[:, None] == levels[None, :]).astype(F32)
    return jnp.sum(onehot * prior_mean[None, :], axis=1)


def shift(v, axis, n, d):
    return lax.ppermute(v, axis, ring(n, d))


def exchange(v):
    return lax.all_to_all(v, "z", split_axis=0, concat_axis=0, tiled=True)


def body(
    embeddings, class_weight, class_bias, propensity, label_ids, label_count, label_bins, prior_mean
):
    width, depth = class_weight.shape
    part = embeddings.shape[0]
    cut = 3 * part // 4
    rest = part - cut
    block = part * NZ
    x_at = lax.axis_index("x")
    offset = (x_at * NZ + lax.axis_index("z")) * width
    bias, prop = class_bias[None, :], propensity[None, :]

    piece = embeddings[cut:]
    own = exchange(jnp.tile(embeddings[:cut], (NZ, 1)))
    side = [piece] + [shift(piece, "x", NX, -d) for d in (1, 2, 3)]
    side = jnp.concatenate(side, axis=0)

    turn = lambda v: lax.dynamic_slice_in_dim(
        jnp.concatenate([v, v], axis=0), x_at * block, v.shape[0], 0
    )
    words = observed_words(turn(label_ids), turn(label_count), offset, width)
    own, words = lax.optimization_barrier((own, words))
    fine = words.reshape(NX, NZ, part, LANES)
    near_words = [fine[d, :, :cut].reshape(NZ * cut, LANES) for d in range(NX)]
    side_words = fine[:, :, cut:].transpose(1, 0, 2, 3).reshape(NX * NZ * rest, LANES)
    front, far, back = (shift(own, "x", NX, -d) for d in (1, 2, 3))
    side = exchange(jnp.tile(side, (NZ, 1)))

    bits = jnp.arange(width // LANES, dtype=jnp.int32)
    seen = (words[:, None, :] >> bits[None, :, None]) & 1
    obs = jnp.sum(seen.astype(F32), axis=0).reshape(1, width)
    prior = bin_prior(label_bins, prior_mean)

    (res0,), post0 = score_call((own,), near_words[:1], class_weight, bias, prop)
    (res1, res3), post1 = score_call(
        (front, back), (near_words[1], near_words[3]), class_weight, bias, prop
    )
    (res2, res_side), post2 = score_call(
        (far, side), (near_words[2], side_words), class_weight, bias, prop
    )
    sums = jnp.concatenate([obs, (post0 + post1) + post2], axis=0)
    sums = sums + shift(sums, "core", NC, 1)
    sums = sum_over_y(sums)
    updated = ((sums[0:1] + 8.0 * prior[None, :]) / (sums[1:2] + 8.0)).reshape(width)

    scaled_weight = (class_weight.astype(F32) / updated[:, None]).astype(BF)

    def term(r):
        return mm(r, scaled_weight, ((1,), (0,)))

    side_parts = exchange(term(res_side).astype(BF))
    moved = []
    for d, r in ((2, res2), (1, res1), (3, res3)):
        moved.append(shift(term(r).astype(BF), "x", NX, d).astype(F32))
    kept = term(res0)

    kept, own_rows = lax.optimization_barrier((kept, own))
    weight_terms = weight_call(
        (side, own_rows, front, far, back), (res_side, res0, res1, res2, res3)
    )
    pairs = pair_blocks(weight_terms.reshape(NY, NC, depth // (NY * NC), width))
    kept, pairs = lax.optimization_barrier((kept, pairs))
    weight_sum = pairs[0].astype(F32)
    for d in (1, 2, 3):
        weight_sum = weight_sum + shift(pairs[d], "y", NY, d).astype(F32)
    weight_grad = (weight_sum / updated[None, :]).astype(BF).T

    near = exchange((kept + moved[0] + moved[1] + moved[2]).astype(BF))
    near = jnp.sum(near.reshape(NZ, cut, depth).astype(F32), axis=0).astype(BF)
    side_sum = jnp.sum(side_parts.reshape(NZ, NX, rest, depth).astype(F32), axis=0)
    last = side_sum[0]
    for d in (1, 2, 3):
        last = last + shift(side_sum[d].astype(BF), "x", NX, d).astype(F32)
    return updated, weight_grad, jnp.concatenate([near, last.astype(BF)], axis=0)


def solution(mesh):
    fine = Mesh(mesh.devices.reshape(NY, NC, NX, NZ), ("y", "core", "x", "z"))
    rows, labels = ("y", "core"), ("x", "z")
    both = rows + labels
    return jax.shard_map(
        body,
        mesh=fine,
        in_specs=(
            P(both, None),
            P(labels, None),
            P(labels),
            P(labels),
            P(rows, None),
            P(rows),
            P(labels),
            P(),
        ),
        out_specs=(P(labels), P(labels, rows), P(both, None)),
        check_vma=False,
    )
```

profile of v0, /device:TPU:16, one launch (start us, length us, event | category | flops | bytes accessed | tf_op | source)
XLA Modules:
  0.0 148.7 jit_solution(5107358002384979962)
XLA Ops:
  2.8 2.7 %collective-permute-start.4 = (bf16[8,768]{1,0:T(8,128)(2,1)S(1)}, bf16[8,768]{1,0:T(8,128)(2,1)S(1)}, u32[]{:S(2)}, u32[]{:S(2)}) collective-permute-start(bf16[8,768]{1,0:T(8,128)(2,1)S(1)} %slice.50), channel_id=1, source_target_pairs={{0,16},{8,24},{16,0},{24,8},{1,17},{9,25},{17,1},{25,9},{2,18},{10... | collective-permute-start | bytes 36872 | tf_op jit(solution)/shard_map/ppermute | solution.py:153
  8.5 8.7 %all-to-all-start = ((bf16[8,24,768]{2,1,0:T(8,128)(2,1)}), bf16[8,24,768]{2,1,0:T(8,128)(2,1)S(1)}, u32[]{:S(2)}, u32[]{:S(2)}) async-start(bf16[8,24,768]{2,1,0:T(8,128)(2,1)} %tile.4), calls=%async_computation | async-start | bytes 589824 | tf_op jit(solution)/shard_map/all_to_all | solution.py:157
  19.9 1.9 %copy.16 = s32[1024,32]{1,0:T(8,128)} copy(s32[1024,32]{0,1:T(8,128)} %get-tuple-element.45) | data formatting | bytes 262144 | tf_op jit(solution)/shard_map/jit(_where)/select_n | solution.py:29
  21.8 1.9 %copy.17 = s32[1024,32]{1,0:T(8,128)} copy(s32[1024,32]{0,1:T(8,128)} %get-tuple-element.46) | data formatting | bytes 262144 | tf_op jit(solution)/shard_map/shift_left | solution.py:30
  23.8 13.1 %select_reduce_fusion = s32[1024,128]{1,0:T(8,128)} fusion(s32[1024,32]{1,0:T(8,128)} %copy.17, s32[1024,32]{1,0:T(8,128)} %copy.16), kind=kLoop, calls=%fused_computation | loop fusion | flops 12451840 | bytes 786432 | tf_op jit(solution)/shard_map/reduce | solution.py:33
  37.7 7.2 %all-to-all-start.1 = ((bf16[8,32,768]{2,1,0:T(8,128)(2,1)}), bf16[8,32,768]{2,1,0:T(8,128)(2,1)}, u32[]{:S(2)}, u32[]{:S(2)}) async-start(bf16[8,32,768]{2,1,0:T(8,128)(2,1)} %tile.5), calls=%async_computation.1 | async-start | bytes 786432 | tf_op jit(solution)/shard_map/all_to_all | solution.py:157
  45.9 2.8 %collective-permute-start = (bf16[192,768]{1,0:T(8,128)(2,1)S(1)}, bf16[192,768]{1,0:T(8,128)(2,1)S(1)}, u32[]{:S(2)}, u32[]{:S(2)}) collective-permute-start(bf16[192,768]{1,0:T(8,128)(2,1)S(1)} %bitcast.47), channel_id=1, source_target_pairs={{0,24},{8,0},{16,8},{24,16},{1,25},{9,1},{17,9},{25,17},{2,26},{10... | collective-permute-start | bytes 884744 | tf_op jit(solution)/shard_map/ppermute | solution.py:153
  50.7 3.1 %scores.3 = (bf16[192,2048]{1,0:T(8,128)(2,1)}, f32[1,2048]{1,0:T(1,128)S(1)}) custom-call(bf16[192,768]{1,0:T(8,128)(2,1)S(1)} %bitcast.48, s32[192,128]{1,0:T(8,128)S(1)} %bitcast.50, bf16[2048,768]{1,0:T(8,128)(2,1)S(1)} %copy-done, f32[1,2048]{1,0:T(1,128)S(1)} %bitcast.55, f32[1,2048]{1,0:T(1,128)S(1)} %bitcast.58), custom_call_target="tpu_custom_call" | custom-call | flops 603979776 | bytes 4227072 | tf_op jit(solution)/shard_map/scores/pallas_call | solution.py:74
  54.5 2.0 %convert_reduce_fusion = f32[16,128]{1,0:T(8,128)} fusion(s32[1024,128]{1,0:T(8,128)S(1)} %copy-done.21), kind=kLoop, calls=%fused_computation.2 | loop fusion | flops 8386560 | bytes 532480 | tf_op jit(solution)/shard_map/reduce_sum | solution.py:190
  56.5 3.3 %collective-permute-done.1.refs_1_.refs_4_ = bf16[192,768]{1,0:T(8,128)(2,1)S(1)} collective-permute-done((bf16[192,768]{1,0:T(8,128)(2,1)S(1)}, bf16[192,768]{1,0:T(8,128)(2,1)S(1)}, u32[]{:S(2)}, u32[]{:S(2)}) %collective-permute-start.1) | collective-permute-done | bytes 294944 | tf_op jit(solution)/shard_map/ppermute | solution.py:153
  59.8 4.1 %scores.4 = (bf16[192,2048]{1,0:T(8,128)(2,1)}, bf16[192,2048]{1,0:T(8,128)(2,1)}, f32[1,2048]{1,0:T(1,128)S(1)}) custom-call(bf16[192,768]{1,0:T(8,128)(2,1)S(1)} %collective-permute-done.refs_0_.refs_2_, bf16[192,768]{1,0:T(8,128)(2,1)S(1)} %collective-permute-done.1.refs_1_.refs_4_, s32[192,128]{1,0:T(8,128)S(1)} %bitcast.54, s32[192,128]{1,0:T(8,128)S(1)} %bitcast.53, ...), custom_call_target="tpu_custom_call" | custom-call | flops 1207959552 | bytes 5308416 | tf_op jit(solution)/shard_map/scores/pallas_call | solution.py:74
  66.8 5.6 %scores.5 = (bf16[192,2048]{1,0:T(8,128)(2,1)}, bf16[256,2048]{1,0:T(8,128)(2,1)}, f32[1,2048]{1,0:T(1,128)S(1)}) custom-call(bf16[192,768]{1,0:T(8,128)(2,1)} %collective-permute-done.2.refs_0_.refs_3_, bf16[256,768]{1,0:T(8,128)(2,1)} %bitcast.8.refs_1_.refs_0_, s32[192,128]{1,0:T(8,128)S(1)} %bitcast.52, s32[256,128]{1,0:T(8,128)S(1)} %bitcast.51, ...), custom_call_target="tpu_custom_call" | custom-call | flops 1409286144 | bytes 5668864 | tf_op jit(solution)/shard_map/scores/pallas_call | solution.py:74
  79.0 2.2 %collective-permute-done.7 = f32[2,2048]{1,0:T(2,128)S(1)} collective-permute-done((f32[2,2048]{1,0:T(2,128)S(1)}, f32[2,2048]{1,0:T(2,128)S(1)}, u32[]{:S(2)}, u32[]{:S(2)}) %collective-permute-start.7) | collective-permute-done | bytes 16416 | tf_op jit(solution)/shard_map/ppermute | solution.py:133
  86.2 5.7 %weights.1 = bf16[768,2048]{1,0:T(8,128)(2,1)S(1)} custom-call(bf16[256,768]{1,0:T(8,128)(2,1)} %bitcast.8.refs_1_.refs_0_, bf16[192,768]{1,0:T(8,128)(2,1)S(1)} %bitcast.49, bf16[192,768]{1,0:T(8,128)(2,1)S(1)} %copy-done.17, bf16[192,768]{1,0:T(8,128)(2,1)} %collective-permute-done.2.refs_0_.refs_3_, bf16[192,768]{1,0:T(8,128)(2,1)S(1)} %copy-done.15, ...), custom_call_target="tpu_custom_call" | custom-call | flops 3221225472 | bytes 8912896 | tf_op jit(solution)/shard_map/weights/pallas_call | solution.py:114
  95.0 6.8 %all-to-all-start.3 = ((bf16[8,32,768]{2,1,0:T(8,128)(2,1)}), bf16[8,32,768]{2,1,0:T(8,128)(2,1)}, u32[]{:S(2)}, u32[]{:S(2)}) async-start(bf16[8,32,768]{2,1,0:T(8,128)(2,1)} %bitcast.63), calls=%async_computation.3 | async-start | bytes 786432 | tf_op jit(solution)/shard_map/all_to_all | solution.py:157
  101.9 3.8 %convolution_convert_fusion.3 = bf16[192,768]{1,0:T(8,128)(2,1)} fusion(bf16[192,2048]{1,0:T(8,128)(2,1)} %get-tuple-element.30.refs_8_, bf16[2048,768]{1,0:T(8,128)(2,1)} %copy-done.19), kind=kOutput, calls=%fused_computation.10 | convolution fusion | flops 604127232 | bytes 4227072 | tf_op jit(solution)/shard_map/dot_general | solution.py:22
  110.3 3.0 %collective-permute-start.16 = (bf16[192,768]{1,0:T(8,128)(2,1)}, bf16[192,768]{1,0:T(8,128)(2,1)}, u32[]{:S(2)}, u32[]{:S(2)}) collective-permute-start(bf16[192,768]{1,0:T(8,128)(2,1)} %convolution_convert_fusion.1), channel_id=1, source_target_pairs={{0,24},{8,0},{16,8},{24,16},{1,25},{9,1},{17,9},{25,17},{2,26},{10... | collective-permute-start | bytes 884744 | tf_op jit(solution)/shard_map/ppermute | solution.py:153
  113.2 4.1 %all-to-all-done.3 = bf16[8,32,768]{2,1,0:T(8,128)(2,1)} async-done(((bf16[8,32,768]{2,1,0:T(8,128)(2,1)}), bf16[8,32,768]{2,1,0:T(8,128)(2,1)}, u32[]{:S(2)}, u32[]{:S(2)}) %all-to-all-start.3) | async-done | bytes 393248 | tf_op jit(solution)/shard_map/all_to_all | solution.py:157
  119.7 2.6 %collective-permute-start.19 = (bf16[8,768]{1,0:T(8,128)(2,1)}, bf16[8,768]{1,0:T(8,128)(2,1)}, u32[]{:S(2)}, u32[]{:S(2)}) collective-permute-start(bf16[8,768]{1,0:T(8,128)(2,1)} %get-tuple-element.48), channel_id=1, source_target_pairs={{0,24},{8,0},{16,8},{24,16},{1,25},{9,1},{17,9},{25,17},{2,26},{10... | collective-permute-start | bytes 36872 | tf_op jit(solution)/shard_map/ppermute | solution.py:153
  122.2 2.0 %fusion = bf16[4,96,2048]{2,1,0:T(8,128)(2,1)S(1)} fusion(bf16[4,96,2048]{2,1,0:T(8,128)(2,1)} %collective-permute-done.10, bf16[4,2,96,2048]{3,2,1,0:T(8,128)(2,1)S(1)} %bitcast.44, s32[]{:T(128)S(6)} %select_n.58), kind=kLoop, calls=%fused_computation.5 | loop fusion | flops 3145728 | bytes 4718596 | tf_op jit(solution)/shard_map/convert_element_type | solution.py:142
  126.5 2.3 %collective-permute-start.13 = (bf16[96,2048]{1,0:T(8,128)(2,1)S(1)}, bf16[96,2048]{1,0:T(8,128)(2,1)S(1)}, u32[]{:S(2)}, u32[]{:S(2)}) collective-permute-start(bf16[96,2048]{1,0:T(8,128)(2,1)S(1)} %get-tuple-element.35), channel_id=1, source_target_pairs={{0,192},{64,0},{128,64},{192,128},{1,193},{65,1},{129,65},{193,129... | collective-permute-start | bytes 1179656 | tf_op jit(solution)/shard_map/ppermute | solution.py:153
  128.8 2.0 %add_convert_fusion = bf16[192,768]{1,0:T(8,128)(2,1)} fusion(bf16[192,768]{1,0:T(8,128)(2,1)} %collective-permute-done.16, bf16[192,768]{1,0:T(8,128)(2,1)} %collective-permute-done.15, f32[192,768]{1,0:T(8,128)S(1)} %copy-done.22, bf16[192,768]{1,0:T(8,128)(2,1)} %collective-permute-done.14), kind=kLoop, calls=%fused_computation.13 | loop fusion | flops 1032192 | bytes 1769472 | tf_op jit(solution)/shard_map/convert_element_type | solution.py:227
  130.8 5.4 %all-to-all-start.2 = ((bf16[8,24,768]{2,1,0:T(8,128)(2,1)}), bf16[8,24,768]{2,1,0:T(8,128)(2,1)S(1)}, u32[]{:S(2)}, u32[]{:S(2)}) async-start(bf16[8,24,768]{2,1,0:T(8,128)(2,1)} %bitcast.22), calls=%async_computation.2 | async-start | bytes 589824 | tf_op jit(solution)/shard_map/all_to_all | solution.py:157
  136.9 6.6 %collective-permute-done.11 = bf16[96,2048]{1,0:T(8,128)(2,1)S(1)} collective-permute-done((bf16[96,2048]{1,0:T(8,128)(2,1)S(1)}, bf16[96,2048]{1,0:T(8,128)(2,1)S(1)}, u32[]{:S(2)}, u32[]{:S(2)}) %collective-permute-start.11) | collective-permute-done | bytes 393248 | tf_op jit(solution)/shard_map/ppermute | solution.py:153
  (122 shorter events, 44.7 us)
Async XLA Ops:
  1.3 35.5 %collective-permute-start.5 = (bf16[8,768]{1,0:T(8,128)(2,1)S(1)}, bf16[8,768]{1,0:T(8,128)(2,1)S(1)}, u32[]{:S(2)}, u32[]{:S(2)}) collective-permute-start(bf16[8,768]{1,0:T(8,128)(2,1)S(1)} %slice.50), channel_id=1, source_target_pairs={{0,8},{8,16},{16,24},{24,0},{1,9},{9,17},{17,25},{25,1},{2,10},{10... | collective-permute-start | bytes 36872 | tf_op jit(solution)/shard_map/ppermute | solution.py:153
  2.8 34.1 %collective-permute-start.4 = (bf16[8,768]{1,0:T(8,128)(2,1)S(1)}, bf16[8,768]{1,0:T(8,128)(2,1)S(1)}, u32[]{:S(2)}, u32[]{:S(2)}) collective-permute-start(bf16[8,768]{1,0:T(8,128)(2,1)S(1)} %slice.50), channel_id=1, source_target_pairs={{0,16},{8,24},{16,0},{24,8},{1,17},{9,25},{17,1},{25,9},{2,18},{10... | collective-permute-start | bytes 36872 | tf_op jit(solution)/shard_map/ppermute | solution.py:153
  5.6 31.3 %collective-permute-start.3 = (bf16[8,768]{1,0:T(8,128)(2,1)S(1)}, bf16[8,768]{1,0:T(8,128)(2,1)S(1)}, u32[]{:S(2)}, u32[]{:S(2)}) collective-permute-start(bf16[8,768]{1,0:T(8,128)(2,1)S(1)} %slice.50), channel_id=1, source_target_pairs={{0,24},{8,0},{16,8},{24,16},{1,25},{9,1},{17,9},{25,17},{2,26},{10... | collective-permute-start | bytes 36872 | tf_op jit(solution)/shard_map/ppermute | solution.py:153
  8.5 28.4 %all-to-all-start = ((bf16[8,24,768]{2,1,0:T(8,128)(2,1)}), bf16[8,24,768]{2,1,0:T(8,128)(2,1)S(1)}, u32[]{:S(2)}, u32[]{:S(2)}) async-start(bf16[8,24,768]{2,1,0:T(8,128)(2,1)} %tile.4), calls=%async_computation | async-start | bytes 589824 | tf_op jit(solution)/shard_map/all_to_all | solution.py:157
  37.7 28.2 %all-to-all-start.1 = ((bf16[8,32,768]{2,1,0:T(8,128)(2,1)}), bf16[8,32,768]{2,1,0:T(8,128)(2,1)}, u32[]{:S(2)}, u32[]{:S(2)}) async-start(bf16[8,32,768]{2,1,0:T(8,128)(2,1)} %tile.5), calls=%async_computation.1 | async-start | bytes 786432 | tf_op jit(solution)/shard_map/all_to_all | solution.py:157
  44.9 21.0 %collective-permute-start.2 = (bf16[192,768]{1,0:T(8,128)(2,1)S(1)}, bf16[192,768]{1,0:T(8,128)(2,1)}, u32[]{:S(2)}, u32[]{:S(2)}) collective-permute-start(bf16[192,768]{1,0:T(8,128)(2,1)S(1)} %bitcast.45), channel_id=1, source_target_pairs={{0,16},{8,24},{16,0},{24,8},{1,17},{9,25},{17,1},{25,9},{2,18},{10... | collective-permute-start | bytes 884744 | tf_op jit(solution)/shard_map/ppermute | solution.py:153
  45.5 14.3 %collective-permute-start.1 = (bf16[192,768]{1,0:T(8,128)(2,1)S(1)}, bf16[192,768]{1,0:T(8,128)(2,1)S(1)}, u32[]{:S(2)}, u32[]{:S(2)}) collective-permute-start(bf16[192,768]{1,0:T(8,128)(2,1)S(1)} %bitcast.46), channel_id=1, source_target_pairs={{0,8},{8,16},{16,24},{24,0},{1,9},{9,17},{17,25},{25,1},{2,10},{10... | collective-permute-start | bytes 884744 | tf_op jit(solution)/shard_map/ppermute | solution.py:153
  45.9 13.9 %collective-permute-start = (bf16[192,768]{1,0:T(8,128)(2,1)S(1)}, bf16[192,768]{1,0:T(8,128)(2,1)S(1)}, u32[]{:S(2)}, u32[]{:S(2)}) collective-permute-start(bf16[192,768]{1,0:T(8,128)(2,1)S(1)} %bitcast.47), channel_id=1, source_target_pairs={{0,24},{8,0},{16,8},{24,16},{1,25},{9,1},{17,9},{25,17},{2,26},{10... | collective-permute-start | bytes 884744 | tf_op jit(solution)/shard_map/ppermute | solution.py:153
  72.5 1.3 collective-permute-start.6
  73.8 3.8 %collective-permute-start.8 = (f32[2,2048]{1,0:T(2,128)S(1)}, f32[2,2048]{1,0:T(2,128)S(1)}, u32[]{:S(2)}, u32[]{:S(2)}) collective-permute-start(f32[2,2048]{1,0:T(2,128)S(1)} %fusion.11), channel_id=1, source_target_pairs={{0,64},{64,128},{128,192},{192,0},{1,65},{65,129},{129,193},{193,1... | collective-permute-start | bytes 49160 | tf_op jit(solution)/shard_map/ppermute | solution.py:133
  75.2 3.8 %collective-permute-start.9 = (f32[2,2048]{1,0:T(2,128)S(1)}, f32[2,2048]{1,0:T(2,128)S(1)}, u32[]{:S(2)}, u32[]{:S(2)}) collective-permute-start(f32[2,2048]{1,0:T(2,128)S(1)} %fusion.11), channel_id=1, source_target_pairs={{0,192},{64,0},{128,64},{192,128},{1,193},{65,1},{129,65},{193,129... | collective-permute-start | bytes 49160 | tf_op jit(solution)/shard_map/ppermute | solution.py:133
  75.9 5.2 %collective-permute-start.7 = (f32[2,2048]{1,0:T(2,128)S(1)}, f32[2,2048]{1,0:T(2,128)S(1)}, u32[]{:S(2)}, u32[]{:S(2)}) collective-permute-start(f32[2,2048]{1,0:T(2,128)S(1)} %fusion.11), channel_id=1, source_target_pairs={{0,128},{64,192},{128,0},{192,64},{1,129},{65,193},{129,1},{193,65... | collective-permute-start | bytes 49160 | tf_op jit(solution)/shard_map/ppermute | solution.py:133
  93.3 26.4 %collective-permute-start.10 = (bf16[4,96,2048]{2,1,0:T(8,128)(2,1)}, bf16[4,96,2048]{2,1,0:T(8,128)(2,1)}, u32[]{:S(2)}, u32[]{:S(2)}) collective-permute-start(bf16[4,96,2048]{2,1,0:T(8,128)(2,1)} %dynamic-slice_bitcast_fusion), channel_id=1, source_target_pairs={{0,32},{32,0},{1,33},{33,1},{2,34},{34,2},{3,35},{35,3},{4,36},{36... | collective-permute-start | bytes 4718600 | tf_op jit(solution)/shard_map/ppermute | solution.py:141
  95.0 22.3 %all-to-all-start.3 = ((bf16[8,32,768]{2,1,0:T(8,128)(2,1)}), bf16[8,32,768]{2,1,0:T(8,128)(2,1)}, u32[]{:S(2)}, u32[]{:S(2)}) async-start(bf16[8,32,768]{2,1,0:T(8,128)(2,1)} %bitcast.63), calls=%async_computation.3 | async-start | bytes 786432 | tf_op jit(solution)/shard_map/all_to_all | solution.py:157
  105.7 18.7 %collective-permute-start.14 = (bf16[192,768]{1,0:T(8,128)(2,1)}, bf16[192,768]{1,0:T(8,128)(2,1)}, u32[]{:S(2)}, u32[]{:S(2)}) collective-permute-start(bf16[192,768]{1,0:T(8,128)(2,1)} %convolution_convert_fusion.3), channel_id=1, source_target_pairs={{0,16},{8,24},{16,0},{24,8},{1,17},{9,25},{17,1},{25,9},{2,18},{10... | collective-permute-start | bytes 884744 | tf_op jit(solution)/shard_map/ppermute | solution.py:153
  108.5 16.1 %collective-permute-start.15 = (bf16[192,768]{1,0:T(8,128)(2,1)}, bf16[192,768]{1,0:T(8,128)(2,1)}, u32[]{:S(2)}, u32[]{:S(2)}) collective-permute-start(bf16[192,768]{1,0:T(8,128)(2,1)} %convolution_convert_fusion.2), channel_id=1, source_target_pairs={{0,8},{8,16},{16,24},{24,0},{1,9},{9,17},{17,25},{25,1},{2,10},{10... | collective-permute-start | bytes 884744 | tf_op jit(solution)/shard_map/ppermute | solution.py:153
  110.3 15.6 %collective-permute-start.16 = (bf16[192,768]{1,0:T(8,128)(2,1)}, bf16[192,768]{1,0:T(8,128)(2,1)}, u32[]{:S(2)}, u32[]{:S(2)}) collective-permute-start(bf16[192,768]{1,0:T(8,128)(2,1)} %convolution_convert_fusion.1), channel_id=1, source_target_pairs={{0,24},{8,0},{16,8},{24,16},{1,25},{9,1},{17,9},{25,17},{2,26},{10... | collective-permute-start | bytes 884744 | tf_op jit(solution)/shard_map/ppermute | solution.py:153
  119.0 7.5 %collective-permute-start.17 = (bf16[8,768]{1,0:T(8,128)(2,1)S(1)}, bf16[8,768]{1,0:T(8,128)(2,1)S(1)}, u32[]{:S(2)}, u32[]{:S(2)}) collective-permute-start(bf16[8,768]{1,0:T(8,128)(2,1)S(1)} %get-tuple-element.47), channel_id=1, source_target_pairs={{0,8},{8,16},{16,24},{24,0},{1,9},{9,17},{17,25},{25,1},{2,10},{10... | collective-permute-start | bytes 36872 | tf_op jit(solution)/shard_map/ppermute | solution.py:153
  119.7 16.5 %collective-permute-start.19 = (bf16[8,768]{1,0:T(8,128)(2,1)}, bf16[8,768]{1,0:T(8,128)(2,1)}, u32[]{:S(2)}, u32[]{:S(2)}) collective-permute-start(bf16[8,768]{1,0:T(8,128)(2,1)} %get-tuple-element.48), channel_id=1, source_target_pairs={{0,24},{8,0},{16,8},{24,16},{1,25},{9,1},{17,9},{25,17},{2,26},{10... | collective-permute-start | bytes 36872 | tf_op jit(solution)/shard_map/ppermute | solution.py:153
  124.4 11.8 %collective-permute-start.18 = (bf16[8,768]{1,0:T(8,128)(2,1)}, bf16[8,768]{1,0:T(8,128)(2,1)S(1)}, u32[]{:S(2)}, u32[]{:S(2)}) collective-permute-start(bf16[8,768]{1,0:T(8,128)(2,1)} %get-tuple-element.49), channel_id=1, source_target_pairs={{0,16},{8,24},{16,0},{24,8},{1,17},{9,25},{17,1},{25,9},{2,18},{10... | collective-permute-start | bytes 36872 | tf_op jit(solution)/shard_map/ppermute | solution.py:153
  124.6 18.9 %collective-permute-start.11 = (bf16[96,2048]{1,0:T(8,128)(2,1)S(1)}, bf16[96,2048]{1,0:T(8,128)(2,1)S(1)}, u32[]{:S(2)}, u32[]{:S(2)}) collective-permute-start(bf16[96,2048]{1,0:T(8,128)(2,1)S(1)} %get-tuple-element.33), channel_id=1, source_target_pairs={{0,64},{64,128},{128,192},{192,0},{1,65},{65,129},{129,193},{193,1... | collective-permute-start | bytes 1179656 | tf_op jit(solution)/shard_map/ppermute | solution.py:153
  125.9 17.6 %collective-permute-start.12 = (bf16[96,2048]{1,0:T(8,128)(2,1)S(1)}, bf16[96,2048]{1,0:T(8,128)(2,1)S(1)}, u32[]{:S(2)}, u32[]{:S(2)}) collective-permute-start(bf16[96,2048]{1,0:T(8,128)(2,1)S(1)} %get-tuple-element.34), channel_id=1, source_target_pairs={{0,128},{64,192},{128,0},{192,64},{1,129},{65,193},{129,1},{193,65... | collective-permute-start | bytes 1179656 | tf_op jit(solution)/shard_map/ppermute | solution.py:153
  126.5 18.8 %collective-permute-start.13 = (bf16[96,2048]{1,0:T(8,128)(2,1)S(1)}, bf16[96,2048]{1,0:T(8,128)(2,1)S(1)}, u32[]{:S(2)}, u32[]{:S(2)}) collective-permute-start(bf16[96,2048]{1,0:T(8,128)(2,1)S(1)} %get-tuple-element.35), channel_id=1, source_target_pairs={{0,192},{64,0},{128,64},{192,128},{1,193},{65,1},{129,65},{193,129... | collective-permute-start | bytes 1179656 | tf_op jit(solution)/shard_map/ppermute | solution.py:153
  130.8 17.2 %all-to-all-start.2 = ((bf16[8,24,768]{2,1,0:T(8,128)(2,1)}), bf16[8,24,768]{2,1,0:T(8,128)(2,1)S(1)}, u32[]{:S(2)}, u32[]{:S(2)}) async-start(bf16[8,24,768]{2,1,0:T(8,128)(2,1)} %bitcast.22), calls=%async_computation.2 | async-start | bytes 589824 | tf_op jit(solution)/shard_map/all_to_all | solution.py:157
  (28 other events, 293.7 us)
where the time goes:
time: 150 us; the launch traced here: 149 us
  starting transfers between devices  53.5 us (36%)
  other arithmetic  26.9 us (18%)
  waiting for transfers between devices  22.2 us (15%)
  Pallas kernels  18.6 us (12%)
  local copies, waits for them, and re-layouts  16.4 us (11%)
  matrix products  10.2 us (7%)
    all_to_all x4, starting transfers between devices, exchange(): return lax.all_to_all(v, 'z', split_axis=0, concat_axis=0, tiled=True)  28.1 us
    ppermute x16, starting transfers between devices, shift(): return lax.ppermute(v, axis, ring(n, d))  21.7 us
    another operation x1, other arithmetic, observed_words(): return lax.reduce(hits, jnp.int32(0), lax.bitwise_or, (1,))  13.1 us
    pallas_call x3, Pallas kernels, score_call(): pl.pallas_call(functools.partial(score_kernel, count=len(xs), chunk=chunk...  12.8 us
    ppermute x16, waiting for transfers between devices, shift(): return lax.ppermute(v, axis, ring(n, d))  12.8 us
    dot_general x5, matrix products, mm(): return lax.dot_general(a, b, (dims, ((), ())), preferred_element_type=F32)  10.2 us
    all_to_all x4, waiting for transfers between devices, exchange(): return lax.all_to_all(v, 'z', split_axis=0, concat_axis=0, tiled=True)  5.74 us
    pallas_call x1, Pallas kernels, weight_call(): pl.pallas_call(functools.partial(weight_kernel, count=len(xs)), grid=(wid...  5.73 us
  transfers between devices with their start and end apart: 24, of which 9 were waited for; matrix products, arithmetic and copies ran while one was open for 28% of the time, Pallas kernels for 5%

commit v1 on v0

v1 whole, which is shorter than its diff:
```python
import functools

import jax
import jax.numpy as jnp
from jax import lax
from jax.experimental import pallas as pl
from jax.experimental.pallas import tpu as pltpu
from jax.sharding import Mesh, PartitionSpec as P

BF = jnp.bfloat16
F32 = jnp.float32
LANES = 128
LOG2E = 1.4426950408889634
NX, NZ, NY, NC = 4, 8, 4, 2


def ring(n, d):
    return [(i, (i + d) % n) for i in range(n)]


def mm(a, b, dims):
    return lax.dot_general(a, b, (dims, ((), ())), preferred_element_type=F32)


def words_kernel(at_ref, ids_ref, count_ref, words_ref, obs_ref, *, width):
    slots, rows = ids_ref.shape
    lanes = lax.broadcasted_iota(jnp.int32, (LANES, LANES), 1)
    slot = lax.broadcasted_iota(jnp.int32, (slots, LANES), 0)
    counts = [jnp.zeros((8, LANES), jnp.int32) for _ in range(width // LANES)]
    for first in range(0, rows, LANES):
        turned = lax.rem(at_ref[1] + first, rows)
        source = pl.ds(pl.multiple_of(turned, LANES), LANES)
        local = ids_ref[:, source] - at_ref[0]
        valid = (slot < count_ref[:, source]) & (local >= 0) & (local < width)
        bit = jnp.left_shift(jnp.int32(256), jnp.where(valid, local >> 7, 0))
        code = jnp.where(valid, bit | (local & (LANES - 1)), 255).T
        words = jnp.zeros((LANES, LANES), jnp.int32)
        for i in range(slots):
            here = jnp.broadcast_to(code[:, i : i + 1], (LANES, LANES))
            words = words | jnp.where((here & 255) == lanes, here >> 8, 0)
        words_ref[first : first + LANES, :] = words
        for b in range(width // LANES):
            hit = (words >> b) & 1
            counts[b] = counts[b] + jnp.sum(hit.reshape(LANES // 8, 8, LANES), axis=0)
    for b in range(width // LANES):
        obs_ref[:, b * LANES : (b + 1) * LANES] = jnp.sum(
            counts[b].astype(F32), axis=0, keepdims=True
        )


def words_call(at, ids, count, width):
    rows = ids.shape[1]
    return pl.pallas_call(
        functools.partial(words_kernel, width=width),
        in_specs=[pl.BlockSpec(memory_space=pltpu.SMEM)] + in_vmem(2),
        out_specs=in_vmem(2),
        out_shape=[
            jax.ShapeDtypeStruct((rows, LANES), jnp.int32),
            jax.ShapeDtypeStruct((1, width), F32),
        ],
        cost_estimate=pl.CostEstimate(
            flops=200 * rows * LANES, bytes_accessed=8 * rows * LANES, transcendentals=0
        ),
        compiler_params=pltpu.CompilerParams(vmem_limit_bytes=16 << 20),
        name="words",
    )(at, ids, count)


def score_kernel(*refs, at, chunk, tile):
    count = len(at)
    x_refs, words_ref = refs[:count], refs[count]
    w_ref, bias_ref, prop_ref = refs[count + 1 : count + 4]
    res_refs, post_ref = refs[count + 4 : -1], refs[-1]
    step = pl.program_id(0)
    cols = pl.ds(pl.multiple_of(step * tile, tile), tile)
    lowest = step * (tile // LANES)
    bias = bias_ref[...] * -LOG2E
    prop = prop_ref[...]
    rest = 1.0 - prop
    total = jnp.zeros((8, tile), F32)
    for x_ref, place, res_ref in zip(x_refs, at, res_refs):
        size = min(chunk, x_ref.shape[0])
        for start in range(0, x_ref.shape[0], size):
            rows = slice(start, start + size)
            scores = mm(x_ref[rows, :], w_ref[cols, :], ((1,), (1,)))
            grown = 1.0 + jnp.exp2(scores * -LOG2E + bias)
            prob = 1.0 / grown
            unseen = rest / (grown - prop)
            words = words_ref[place + start : place + start + size, :]
            seen = jnp.concatenate(
                [words & jnp.left_shift(jnp.int32(1), lowest + b) for b in range(tile // LANES)],
                axis=1,
            )
            posterior = jnp.where(seen != 0, 1.0, unseen)
            res_ref[rows, :] = (prob - posterior).astype(BF)
            total = total + jnp.sum(posterior.reshape(size // 8, 8, tile), axis=0)
    post_ref[...] = jnp.sum(total, axis=0, keepdims=True)


def in_vmem(count):
    return [pl.BlockSpec(memory_space=pltpu.VMEM)] * count


def score_call(xs, at, words, w, bias, prop, chunk=256, tile=512):
    width, depth = w.shape
    rows = sum(x.shape[0] for x in xs)
    narrow = pl.BlockSpec((1, tile), lambda i: (0, i))
    *res, post = pl.pallas_call(
        functools.partial(score_kernel, at=at, chunk=chunk, tile=tile),
        grid=(width // tile,),
        in_specs=in_vmem(len(xs) + 2) + [narrow, narrow],
        out_specs=[pl.BlockSpec((x.shape[0], tile), lambda i: (0, i)) for x in xs] + [narrow],
        out_shape=[pltpu.HBM((x.shape[0], width), BF) for x in xs]
        + [jax.ShapeDtypeStruct((1, width), F32)],
        cost_estimate=pl.CostEstimate(
            flops=2 * rows * width * depth,
            bytes_accessed=2 * (rows * depth + width * depth + rows * width),
            transcendentals=3 * rows * width,
        ),
        compiler_params=pltpu.CompilerParams(vmem_limit_bytes=24 << 20),
        name="scores",
    )(*xs, words, w, bias, prop)
    return res, post


def weight_kernel(core_ref, *refs, count):
    x_refs, r_refs = refs[:count], refs[count : 2 * count]
    kept_ref, given_ref, x_all, r_all, out = refs[2 * count :]
    mine = core_ref[0]

    @pl.when(pl.program_id(0) == 0)
    def _():
        at = 0
        for x_ref in x_refs:
            x_all[at : at + x_ref.shape[0], :] = x_ref[...]
            at += x_ref.shape[0]

    at = 0
    for r_ref in r_refs:
        r_all[at : at + r_ref.shape[0], :] = r_ref[...]
        at += r_ref.shape[0]
    out[...] = mm(x_all[...], r_all[...], ((0,), (0,))).astype(BF)
    step = kept_ref.shape[1]
    for y in range(NY):
        kept_ref[y] = out[pl.ds(pl.multiple_of((y * NC + mine) * step, step), step), :]
        given_ref[y] = out[pl.ds(pl.multiple_of((y * NC + 1 - mine) * step, step), step), :]


def weight_call(core, xs, rs, tile=512):
    depth = xs[0].shape[1]
    width = rs[0].shape[1]
    rows = sum(x.shape[0] for x in xs)
    step = depth // (NY * NC)
    half = pl.BlockSpec((NY, step, tile), lambda i: (0, 0, i))
    return pl.pallas_call(
        functools.partial(weight_kernel, count=len(xs)),
        grid=(width // tile,),
        in_specs=[pl.BlockSpec(memory_space=pltpu.SMEM)]
        + [pl.BlockSpec(x.shape, lambda i: (0, 0)) for x in xs]
        + [pl.BlockSpec((r.shape[0], tile), lambda i: (0, i)) for r in rs],
        out_specs=[half, half],
        out_shape=[pltpu.HBM((NY, step, width), BF)] * 2,
        scratch_shapes=[
            pltpu.VMEM((rows, depth), BF),
            pltpu.VMEM((rows, tile), BF),
            pltpu.VMEM((depth, tile), BF),
        ],
        cost_estimate=pl.CostEstimate(
            flops=2 * rows * width * depth,
            bytes_accessed=2 * (rows * (depth + width) + width * depth),
            transcendentals=0,
        ),
        compiler_params=pltpu.CompilerParams(vmem_limit_bytes=60 << 20),
        name="weights",
    )(core, *xs, *rs)


def bin_prior(bins, prior_mean):
    levels = jnp.arange(prior_mean.shape[0], dtype=jnp.int32)
    onehot = (bins[:, None] == levels[None, :]).astype(F32)
    return jnp.sum(onehot * prior_mean[None, :], axis=1)


def shift(v, axis, n, d):
    return lax.ppermute(v, axis, ring(n, d))


def exchange(v, axis):
    return lax.all_to_all(v, axis, split_axis=0, concat_axis=0, tiled=True)


def body(
    embeddings, class_weight, class_bias, propensity, label_ids, label_count, label_bins, prior_mean
):
    width, depth = class_weight.shape
    part = embeddings.shape[0]
    block = part * NZ
    x_at, core, y = (lax.axis_index(a) for a in ("x", "core", "y"))
    offset = (x_at * NZ + lax.axis_index("z")) * width
    bias, prop = class_bias[None, :], propensity[None, :]

    own = exchange(jnp.tile(embeddings, (NZ, 1)), "z")
    at = jnp.stack([offset, x_at * block])
    words, obs = words_call(at, label_ids.T, label_count[None, :], width)
    prior = bin_prior(label_bins, prior_mean)

    def brought(d):
        return shift(own, "x", NX, -d)

    front, back, far = brought(1), brought(3), brought(2)
    (res0,), post0 = score_call((own,), (0,), words, class_weight, bias, prop)
    (res1,), post1 = score_call((front,), (block,), words, class_weight, bias, prop)
    (res3,), post3 = score_call((back,), (3 * block,), words, class_weight, bias, prop)
    (res2,), post2 = score_call((far,), (2 * block,), words, class_weight, bias, prop)
    post = (post0 + post1) + (post3 + post2)
    both = jnp.concatenate([obs, post], axis=0)[None]
    sums = jnp.sum(exchange(jnp.tile(both, (NY * NC, 1, 1)), ("y", "core")), axis=0)
    updated = ((sums[0:1] + 8.0 * prior[None, :]) / (sums[1:2] + 8.0)).reshape(width)

    kept_rows, given = weight_call(core[None], (own, front, far, back), (res0, res1, res2, res3))
    pair = kept_rows.astype(F32) + shift(given, "core", NC, 1).astype(F32)
    pair = pair.astype(BF)
    pairs = [lax.dynamic_index_in_dim(pair, (y + d) % NY, 0, keepdims=False) for d in range(NY)]

    scaled_weight = (class_weight.astype(F32) / updated[:, None]).astype(BF)

    def term(r):
        return mm(r, scaled_weight, ((1,), (0,)))

    moved = []
    for d, r in ((2, res2), (1, res1), (3, res3)):
        moved.append(shift(term(r).astype(BF), "x", NX, d).astype(F32))
    kept = term(res0)
    kept, pairs = lax.optimization_barrier((kept, pairs))
    weight_sum = pairs[0].astype(F32)
    for d in (1, 2, 3):
        weight_sum = weight_sum + shift(pairs[d], "y", NY, d).astype(F32)
    weight_grad = (weight_sum / updated[None, :]).astype(BF).T

    parts = exchange((kept + moved[0] + moved[1] + moved[2]).astype(BF), "z")
    embed_grad = jnp.sum(parts.reshape(NZ, part, depth).astype(F32), axis=0).astype(BF)
    return updated, weight_grad, embed_grad


def solution(mesh):
    fine = Mesh(mesh.devices.reshape(NY, NC, NX, NZ), ("y", "core", "x", "z"))
    rows, labels = ("y", "core"), ("x", "z")
    both = rows + labels
    return jax.shard_map(
        body,
        mesh=fine,
        in_specs=(
            P(both, None),
            P(labels, None),
            P(labels),
            P(labels),
            P(rows, None),
            P(rows),
            P(labels),
            P(),
        ),
        out_specs=(P(labels), P(labels, rows), P(both, None)),
        check_vma=False,
    )
```

time: 150 us -> 117 us (0.78)
  starting transfers between devices: 53.5 us -> 29.3 us
  other arithmetic: 26.9 us -> 6.29 us
  waiting for transfers between devices: 22.2 us -> 38 us
  Pallas kernels: 18.6 us -> 28.8 us
  local copies, waits for them, and re-layouts: 16.4 us -> 7.95 us
  matrix products: 10.2 us -> 3.92 us
    all_to_all x4 -> x3, waiting for transfers between devices: 5.74 us -> 23.9 us  [exchange(): return lax.all_to_all(v, axis, split_axis=0, concat_axis=0, tiled=True)]
    another operation x2 -> x1, other arithmetic: 13.1 us -> 0.07 us  [body(): at = jnp.stack([offset, x_at * block])]
    all_to_all x4 -> x3, starting transfers between devices: 28.1 us -> 16.7 us  [exchange(): return lax.all_to_all(v, axis, split_axis=0, concat_axis=0, tiled=True)]
    ppermute x16 -> x10, starting transfers between devices: 21.7 us -> 12.6 us  [shift(): return lax.ppermute(v, axis, ring(n, d))]
    pallas_call x3 -> x5, Pallas kernels: 12.8 us -> 21.2 us  [the longest x4 15.1 us: score_call(): pl.pallas_call(functools.partial(score_kernel, at=at, chunk=chunk, tile=t...]
    dot_general x5 -> x4, matrix products: 10.2 us -> 3.92 us  [mm(): return lax.dot_general(a, b, (dims, ((), ())), preferred_element_type=F32)]
    ppermute x4 -> x0, waiting for transfers between devices: 3.69 us -> none  [the longest x3 3.69 us: sum_over_y(): one, two, three = (lax.ppermute(v, 'y', ring(NY, d)) for d in (1, 2, 3))]
    ppermute x4 -> x0, starting transfers between devices: 3.66 us -> none  [the longest x3 3.66 us: sum_over_y(): one, two, three = (lax.ppermute(v, 'y', ring(NY, d)) for d in (1, 2, 3))]
  transfers between devices with their start and end apart: 24 -> 13, of which waited for: 9 -> 6; matrix products, arithmetic and copies ran while one was open for 28% -> 8% of each run, Pallas kernels for 5% -> 22%
where the time goes in v1:
time: 117 us; the launch traced here: 115 us
  waiting for transfers between devices  38 us (32%)
  starting transfers between devices  29.3 us (25%)
  Pallas kernels  28.8 us (25%)
  local copies, waits for them, and re-layouts  7.95 us (7%)
  other arithmetic  6.29 us (5%)
  matrix products  3.92 us (3%)
    all_to_all x3, waiting for transfers between devices, exchange(): return lax.all_to_all(v, axis, split_axis=0, concat_axis=0, tiled=True)  23.9 us
    all_to_all x3, starting transfers between devices, exchange(): return lax.all_to_all(v, axis, split_axis=0, concat_axis=0, tiled=True)  16.7 us
    pallas_call x4, Pallas kernels, score_call(): pl.pallas_call(functools.partial(score_kernel, at=at, chunk=chunk, tile=t...  15.1 us
    ppermute x10, waiting for transfers between devices, shift(): return lax.ppermute(v, axis, ring(n, d))  14.1 us
    ppermute x10, starting transfers between devices, shift(): return lax.ppermute(v, axis, ring(n, d))  12.6 us
    pallas_call x1, Pallas kernels, weight_call(): pl.pallas_call(functools.partial(weight_kernel, count=len(xs)), grid=(wid...  7.57 us
    pallas_call x1, Pallas kernels, words_call(): pl.pallas_call(functools.partial(words_kernel, width=width), in_specs=[pl...  6.19 us
    unnamed x28, local copies, waits for them, and re-layouts  5.57 us
  transfers between devices with their start and end apart: 13, of which 6 were waited for; matrix products, arithmetic and copies ran while one was open for 8% of the time, Pallas kernels for 22%

profile of v1, /device:TPU:16, one launch (start us, length us, event | category | flops | bytes accessed | tf_op | source)
XLA Modules:
  0.0 115.1 jit_solution(2684723669036244903)
XLA Ops:
  0.6 1.6 %tile.4 = bf16[8,32,768]{2,1,0:T(8,128)(2,1)} broadcast(bf16[32,768]{1,0:T(8,128)(2,1)} %param.8), dimensions={1,2} | broadcast | bytes 442368 | tf_op jit(solution)/shard_map/tile | solution.py:202
  2.2 8.5 %all-to-all-start = ((bf16[8,32,768]{2,1,0:T(8,128)(2,1)}), bf16[8,32,768]{2,1,0:T(8,128)(2,1)S(1)}, u32[]{:S(2)}, u32[]{:S(2)}) async-start(bf16[8,32,768]{2,1,0:T(8,128)(2,1)} %tile.4), calls=%async_computation | async-start | bytes 786432 | tf_op jit(solution)/shard_map/all_to_all | solution.py:189
  11.5 13.9 %all-to-all-done = bf16[8,32,768]{2,1,0:T(8,128)(2,1)S(1)} async-done(((bf16[8,32,768]{2,1,0:T(8,128)(2,1)}), bf16[8,32,768]{2,1,0:T(8,128)(2,1)S(1)}, u32[]{:S(2)}, u32[]{:S(2)}) %all-to-all-start) | async-done | bytes 393248 | tf_op jit(solution)/shard_map/all_to_all | solution.py:189
  25.4 3.0 %collective-permute-start.2 = (bf16[256,768]{1,0:T(8,128)(2,1)S(1)}, bf16[256,768]{1,0:T(8,128)(2,1)}, u32[]{:S(2)}, u32[]{:S(2)}) collective-permute-start(bf16[256,768]{1,0:T(8,128)(2,1)S(1)} %bitcast.29), channel_id=1, source_target_pairs={{0,16},{8,24},{16,0},{24,8},{1,17},{9,25},{17,1},{25,9},{2,18},{10... | collective-permute-start | bytes 1179656 | tf_op jit(solution)/shard_map/ppermute | solution.py:185
  30.6 6.2 %words.1 = (s32[1024,128]{1,0:T(8,128)S(1)}, f32[1,2048]{1,0:T(1,128)S(1)}) custom-call(s32[2]{0:T(128)S(1)} %pad_add_fusion.at_ref, s32[32,1024]{1,0:T(8,128)S(1)} %bitcast.42, s32[1,1024]{1,0:T(1,128)S(1)} %bitcast.43), custom_call_target="tpu_custom_call" | custom-call | flops 26214400 | bytes 1048576 | tf_op jit(solution)/shard_map/words/pallas_call | solution.py:53
  36.8 2.7 %collective-permute-start = (bf16[256,768]{1,0:T(8,128)(2,1)S(1)}, bf16[256,768]{1,0:T(8,128)(2,1)S(1)}, u32[]{:S(2)}, u32[]{:S(2)}) collective-permute-start(bf16[256,768]{1,0:T(8,128)(2,1)S(1)} %bitcast.31), channel_id=1, source_target_pairs={{0,24},{8,0},{16,8},{24,16},{1,25},{9,1},{17,9},{25,17},{2,26},{10... | collective-permute-start | bytes 1179656 | tf_op jit(solution)/shard_map/ppermute | solution.py:185
  39.6 1.9 %copy-done = bf16[2048,768]{1,0:T(8,128)(2,1)S(1)} copy-done((bf16[2048,768]{1,0:T(8,128)(2,1)S(1)}, bf16[2048,768]{1,0:T(8,128)(2,1)}, u32[]{:S(2)}) %copy-start) | copy-done | bytes 3145752
  42.9 3.3 %scores.4 = (bf16[256,2048]{1,0:T(8,128)(2,1)}, f32[1,2048]{1,0:T(1,128)S(1)}) custom-call(bf16[256,768]{1,0:T(8,128)(2,1)S(1)} %bitcast.32, s32[1024,128]{1,0:T(8,128)S(1)} %get-tuple-element.21.refs_1_, bf16[2048,768]{1,0:T(8,128)(2,1)S(1)} %copy-done, f32[1,2048]{1,0:T(1,128)S(1)} %bitcast.34, f32[1,2048]{1,0:T(1,128)S(1)} %bitcast.38), custom_call_target="tpu_custom_call" | custom-call | flops 805306368 | bytes 4587520 | tf_op jit(solution)/shard_map/scores/pallas_call | solution.py:108
  46.1 4.2 %scores.7 = (bf16[256,2048]{1,0:T(8,128)(2,1)}, f32[1,2048]{1,0:T(1,128)S(1)}) custom-call(bf16[256,768]{1,0:T(8,128)(2,1)} %collective-permute-done.2.refs_0_.refs_2_, s32[1024,128]{1,0:T(8,128)S(1)} %get-tuple-element.21.refs_1_, bf16[2048,768]{1,0:T(8,128)(2,1)S(1)} %copy-done, f32[1,2048]{1,0:T(1,128)S(1)} %bitcast.35, f32[1,2048]{1,0:T(1,128)S(1)} %bitcast.39), custom_call_target="tpu_custom_call" | custom-call | flops 805306368 | bytes 4587520 | tf_op jit(solution)/shard_map/scores/pallas_call | solution.py:108
  50.4 4.3 %scores.6 = (bf16[256,2048]{1,0:T(8,128)(2,1)}, f32[1,2048]{1,0:T(1,128)S(1)}) custom-call(bf16[256,768]{1,0:T(8,128)(2,1)} %collective-permute-done.1.refs_0_.refs_3_, s32[1024,128]{1,0:T(8,128)S(1)} %get-tuple-element.21.refs_1_, bf16[2048,768]{1,0:T(8,128)(2,1)S(1)} %copy-done.1, f32[1,2048]{1,0:T(1,128)S(1)} %bitcast.36, f32[1,2048]{1,0:T(1,128)S(1)} %bitcast.40), custom_call_target="tpu_custom_call" | custom-call | flops 805306368 | bytes 4587520 | tf_op jit(solution)/shard_map/scores/pallas_call | solution.py:108
  54.7 3.2 %scores.5 = (bf16[256,2048]{1,0:T(8,128)(2,1)}, f32[1,2048]{1,0:T(1,128)S(1)}) custom-call(bf16[256,768]{1,0:T(8,128)(2,1)S(1)} %collective-permute-done.refs_0_.refs_1_, s32[1024,128]{1,0:T(8,128)S(1)} %get-tuple-element.21.refs_1_, bf16[2048,768]{1,0:T(8,128)(2,1)S(1)} %copy-done.1, f32[1,2048]{1,0:T(1,128)S(1)} %bitcast.37, f32[1,2048]{1,0:T(1,128)S(1)} %bitcast.41), custom_call_target="tpu_custom_call" | custom-call | flops 805306368 | bytes 4587520 | tf_op jit(solution)/shard_map/scores/pallas_call | solution.py:108
  58.7 4.8 %all-to-all-start.1 = ((f32[8,2,2048]{2,1,0:T(2,128)}), f32[8,2,2048]{2,1,0:T(2,128)S(1)}, u32[]{:S(2)}, u32[]{:S(2)}) async-start(f32[8,2,2048]{2,1,0:T(2,128)} %tile.5), calls=%async_computation.1 | async-start | bytes 262144 | tf_op jit(solution)/shard_map/all_to_all | solution.py:189
  63.5 7.6 %weights.1 = (bf16[4,96,2048]{2,1,0:T(8,128)(2,1)}, bf16[4,96,2048]{2,1,0:T(8,128)(2,1)}) custom-call(s32[1]{0:T(128)} %bitcast.9.core_ref, bf16[256,768]{1,0:T(8,128)(2,1)} %bitcast.33, bf16[256,768]{1,0:T(8,128)(2,1)} %copy-done.3, bf16[256,768]{1,0:T(8,128)(2,1)} %collective-permute-done.2.refs_0_.refs_2_, ...), custom_call_target="tpu_custom_call" | custom-call | flops 3221225472 | bytes 8912896 | tf_op jit(solution)/shard_map/weights/pallas_call | solution.py:155
  72.5 1.0 convolution_convert_fusion.2
  76.5 2.6 %collective-permute-start.9 = (bf16[256,768]{1,0:T(8,128)(2,1)S(1)}, bf16[256,768]{1,0:T(8,128)(2,1)S(1)}, u32[]{:S(2)}, u32[]{:S(2)}) collective-permute-start(bf16[256,768]{1,0:T(8,128)(2,1)S(1)} %convolution_convert_fusion), channel_id=1, source_target_pairs={{0,24},{8,0},{16,8},{24,16},{1,25},{9,1},{17,9},{25,17},{2,26},{10... | collective-permute-start | bytes 1179656 | tf_op jit(solution)/shard_map/ppermute | solution.py:185
  80.1 2.0 %add_convert_fusion = bf16[4,96,2048]{2,1,0:T(8,128)(2,1)S(1)} fusion(bf16[4,96,2048]{2,1,0:T(8,128)(2,1)} %collective-permute-done.3, bf16[4,96,2048]{2,1,0:T(8,128)(2,1)S(1)} %copy-done.8), kind=kLoop, calls=%fused_computation.1 | loop fusion | flops 3145728 | bytes 4718592 | tf_op jit(solution)/shard_map/convert_element_type | solution.py:222
  82.3 1.2 %collective-permute-start.4 = (bf16[96,2048]{1,0:T(8,128)(2,1)S(1)}, bf16[96,2048]{1,0:T(8,128)(2,1)S(1)}, u32[]{:S(2)}, u32[]{:S(2)}) collective-permute-start(bf16[96,2048]{1,0:T(8,128)(2,1)S(1)} %get-tuple-element.33), channel_id=1, source_target_pairs={{0,64},{64,128},{128,192},{192,0},{1,65},{65,129},{129,193},{193,1... | collective-permute-start | bytes 1179656 | tf_op jit(solution)/shard_map/ppermute | solution.py:185
  84.4 2.8 %collective-permute-done.7 = bf16[256,768]{1,0:T(8,128)(2,1)S(1)} collective-permute-done((bf16[256,768]{1,0:T(8,128)(2,1)S(1)}, bf16[256,768]{1,0:T(8,128)(2,1)S(1)}, u32[]{:S(2)}, u32[]{:S(2)}) %collective-permute-start.7) | collective-permute-done | bytes 393248 | tf_op jit(solution)/shard_map/ppermute | solution.py:185
  87.7 7.2 %collective-permute-done.8 = bf16[256,768]{1,0:T(8,128)(2,1)S(1)} collective-permute-done((bf16[256,768]{1,0:T(8,128)(2,1)S(1)}, bf16[256,768]{1,0:T(8,128)(2,1)S(1)}, u32[]{:S(2)}, u32[]{:S(2)}) %collective-permute-start.8) | collective-permute-done | bytes 393248 | tf_op jit(solution)/shard_map/ppermute | solution.py:185
  95.9 3.5 %all-to-all-start.2 = ((bf16[8,32,768]{2,1,0:T(8,128)(2,1)}), bf16[8,32,768]{2,1,0:T(8,128)(2,1)S(1)}, u32[]{:S(2)}, u32[]{:S(2)}) async-start(bf16[8,32,768]{2,1,0:T(8,128)(2,1)} %bitcast.15), calls=%async_computation.2 | async-start | bytes 786432 | tf_op jit(solution)/shard_map/all_to_all | solution.py:189
  99.3 2.3 %collective-permute-done.5 = bf16[96,2048]{1,0:T(8,128)(2,1)S(1)} collective-permute-done((bf16[96,2048]{1,0:T(8,128)(2,1)S(1)}, bf16[96,2048]{1,0:T(8,128)(2,1)S(1)}, u32[]{:S(2)}, u32[]{:S(2)}) %collective-permute-start.5) | collective-permute-done | bytes 393248 | tf_op jit(solution)/shard_map/ppermute | solution.py:185
  101.6 1.8 %collective-permute-done.6 = bf16[96,2048]{1,0:T(8,128)(2,1)S(1)} collective-permute-done((bf16[96,2048]{1,0:T(8,128)(2,1)S(1)}, bf16[96,2048]{1,0:T(8,128)(2,1)S(1)}, u32[]{:S(2)}, u32[]{:S(2)}) %collective-permute-start.6) | collective-permute-done | bytes 393248 | tf_op jit(solution)/shard_map/ppermute | solution.py:185
  103.4 1.0 fusion
  104.4 10.0 %all-to-all-done.2 = bf16[8,32,768]{2,1,0:T(8,128)(2,1)S(1)} async-done(((bf16[8,32,768]{2,1,0:T(8,128)(2,1)}), bf16[8,32,768]{2,1,0:T(8,128)(2,1)S(1)}, u32[]{:S(2)}, u32[]{:S(2)}) %all-to-all-start.2) | async-done | bytes 393248 | tf_op jit(solution)/shard_map/all_to_all | solution.py:189
  (55 shorter events, 13.8 us)
Async XLA Ops:
  2.2 23.2 %all-to-all-start = ((bf16[8,32,768]{2,1,0:T(8,128)(2,1)}), bf16[8,32,768]{2,1,0:T(8,128)(2,1)S(1)}, u32[]{:S(2)}, u32[]{:S(2)}) async-start(bf16[8,32,768]{2,1,0:T(8,128)(2,1)} %tile.4), calls=%async_computation | async-start | bytes 786432 | tf_op jit(solution)/shard_map/all_to_all | solution.py:189
  25.4 25.0 %copy-start.2 = (bf16[8,32,768]{2,1,0:T(8,128)(2,1)}, bf16[8,32,768]{2,1,0:T(8,128)(2,1)S(1)}, u32[]{:S(2)}) copy-start(bf16[8,32,768]{2,1,0:T(8,128)(2,1)S(1)} %all-to-all-done) | copy-start | bytes 1179652
  25.4 20.8 %collective-permute-start.2 = (bf16[256,768]{1,0:T(8,128)(2,1)S(1)}, bf16[256,768]{1,0:T(8,128)(2,1)}, u32[]{:S(2)}, u32[]{:S(2)}) collective-permute-start(bf16[256,768]{1,0:T(8,128)(2,1)S(1)} %bitcast.29), channel_id=1, source_target_pairs={{0,16},{8,24},{16,0},{24,8},{1,17},{9,25},{17,1},{25,9},{2,18},{10... | collective-permute-start | bytes 1179656 | tf_op jit(solution)/shard_map/ppermute | solution.py:185
  28.4 22.0 %collective-permute-start.1 = (bf16[256,768]{1,0:T(8,128)(2,1)S(1)}, bf16[256,768]{1,0:T(8,128)(2,1)}, u32[]{:S(2)}, u32[]{:S(2)}) collective-permute-start(bf16[256,768]{1,0:T(8,128)(2,1)S(1)} %bitcast.30), channel_id=1, source_target_pairs={{0,8},{8,16},{16,24},{24,0},{1,9},{9,17},{17,25},{25,1},{2,10},{10... | collective-permute-start | bytes 1179656 | tf_op jit(solution)/shard_map/ppermute | solution.py:185
  29.0 0.9 copy-start.6
  36.8 17.8 %collective-permute-start = (bf16[256,768]{1,0:T(8,128)(2,1)S(1)}, bf16[256,768]{1,0:T(8,128)(2,1)S(1)}, u32[]{:S(2)}, u32[]{:S(2)}) collective-permute-start(bf16[256,768]{1,0:T(8,128)(2,1)S(1)} %bitcast.31), channel_id=1, source_target_pairs={{0,24},{8,0},{16,8},{24,16},{1,25},{9,1},{17,9},{25,17},{2,26},{10... | collective-permute-start | bytes 1179656 | tf_op jit(solution)/shard_map/ppermute | solution.py:185
  39.6 1.9 %copy-start = (bf16[2048,768]{1,0:T(8,128)(2,1)S(1)}, bf16[2048,768]{1,0:T(8,128)(2,1)}, u32[]{:S(2)}) copy-start(bf16[2048,768]{1,0:T(8,128)(2,1)} %refs_2_.7) | copy-start | bytes 9437188
  42.9 7.5 %copy-start.1 = (bf16[2048,768]{1,0:T(8,128)(2,1)S(1)}, bf16[2048,768]{1,0:T(8,128)(2,1)}, u32[]{:S(2)}) copy-start(bf16[2048,768]{1,0:T(8,128)(2,1)} %refs_2_.7) | copy-start | bytes 9437188
  54.7 3.3 %copy-start.3 = (bf16[256,768]{1,0:T(8,128)(2,1)}, bf16[256,768]{1,0:T(8,128)(2,1)S(1)}, u32[]{:S(2)}) copy-start(bf16[256,768]{1,0:T(8,128)(2,1)S(1)} %collective-permute-done.refs_0_.refs_1_) | copy-start | bytes 1179652
  58.7 12.5 %all-to-all-start.1 = ((f32[8,2,2048]{2,1,0:T(2,128)}), f32[8,2,2048]{2,1,0:T(2,128)S(1)}, u32[]{:S(2)}, u32[]{:S(2)}) async-start(f32[8,2,2048]{2,1,0:T(2,128)} %tile.5), calls=%async_computation.1 | async-start | bytes 262144 | tf_op jit(solution)/shard_map/all_to_all | solution.py:189
  71.0 9.1 %collective-permute-start.3 = (bf16[4,96,2048]{2,1,0:T(8,128)(2,1)}, bf16[4,96,2048]{2,1,0:T(8,128)(2,1)}, u32[]{:S(2)}, u32[]{:S(2)}) collective-permute-start(bf16[4,96,2048]{2,1,0:T(8,128)(2,1)} %get-tuple-element.31), channel_id=1, source_target_pairs={{0,32},{32,0},{1,33},{33,1},{2,34},{34,2},{3,35},{35,3},{4,36},{36... | collective-permute-start | bytes 4718600 | tf_op jit(solution)/shard_map/ppermute | solution.py:185
  71.2 32.2 %copy-start.9 = (f32[1,2048]{1,0:T(1,128)}, f32[1,2048]{1,0:T(1,128)S(1)}, u32[]{:S(2)}) copy-start(f32[1,2048]{1,0:T(1,128)S(1)} %fusion.1) | copy-start | bytes 24580
  71.3 1.2 %copy-start.12 = (bf16[256,2048]{1,0:T(8,128)(2,1)S(1)}, bf16[256,2048]{1,0:T(8,128)(2,1)}, u32[]{:S(2)}) copy-start(bf16[256,2048]{1,0:T(8,128)(2,1)} %get-tuple-element.28.refs_6_) | copy-start | bytes 3145732
  72.5 1.2 %copy-start.13 = (bf16[256,2048]{1,0:T(8,128)(2,1)S(1)}, bf16[256,2048]{1,0:T(8,128)(2,1)}, u32[]{:S(2)}) copy-start(bf16[256,2048]{1,0:T(8,128)(2,1)} %get-tuple-element.27.refs_5_) | copy-start | bytes 3145732
  73.5 2.1 %copy-start.11 = (bf16[256,2048]{1,0:T(8,128)(2,1)S(1)}, bf16[256,2048]{1,0:T(8,128)(2,1)}, u32[]{:S(2)}) copy-start(bf16[256,2048]{1,0:T(8,128)(2,1)} %get-tuple-element.29.refs_7_) | copy-start | bytes 3145732
  73.5 13.6 %collective-permute-start.7 = (bf16[256,768]{1,0:T(8,128)(2,1)S(1)}, bf16[256,768]{1,0:T(8,128)(2,1)S(1)}, u32[]{:S(2)}, u32[]{:S(2)}) collective-permute-start(bf16[256,768]{1,0:T(8,128)(2,1)S(1)} %convolution_convert_fusion.2), channel_id=1, source_target_pairs={{0,16},{8,24},{16,0},{24,8},{1,17},{9,25},{17,1},{25,9},{2,18},{10... | collective-permute-start | bytes 1179656 | tf_op jit(solution)/shard_map/ppermute | solution.py:185
  74.7 4.4 %copy-start.10 = (bf16[256,2048]{1,0:T(8,128)(2,1)S(1)}, bf16[256,2048]{1,0:T(8,128)(2,1)}, u32[]{:S(2)}) copy-start(bf16[256,2048]{1,0:T(8,128)(2,1)} %get-tuple-element.26.refs_4_) | copy-start | bytes 3145732
  74.7 20.2 %collective-permute-start.8 = (bf16[256,768]{1,0:T(8,128)(2,1)S(1)}, bf16[256,768]{1,0:T(8,128)(2,1)S(1)}, u32[]{:S(2)}, u32[]{:S(2)}) collective-permute-start(bf16[256,768]{1,0:T(8,128)(2,1)S(1)} %convolution_convert_fusion.1), channel_id=1, source_target_pairs={{0,8},{8,16},{16,24},{24,0},{1,9},{9,17},{17,25},{25,1},{2,10},{10... | collective-permute-start | bytes 1179656 | tf_op jit(solution)/shard_map/ppermute | solution.py:185
  76.5 3.6 %copy-start.8 = (bf16[4,96,2048]{2,1,0:T(8,128)(2,1)S(1)}, bf16[4,96,2048]{2,1,0:T(8,128)(2,1)}, u32[]{:S(2)}) copy-start(bf16[4,96,2048]{2,1,0:T(8,128)(2,1)} %get-tuple-element.30) | copy-start | bytes 4718596
  76.5 18.4 %collective-permute-start.9 = (bf16[256,768]{1,0:T(8,128)(2,1)S(1)}, bf16[256,768]{1,0:T(8,128)(2,1)S(1)}, u32[]{:S(2)}, u32[]{:S(2)}) collective-permute-start(bf16[256,768]{1,0:T(8,128)(2,1)S(1)} %convolution_convert_fusion), channel_id=1, source_target_pairs={{0,24},{8,0},{16,8},{24,16},{1,25},{9,1},{17,9},{25,17},{2,26},{10... | collective-permute-start | bytes 1179656 | tf_op jit(solution)/shard_map/ppermute | solution.py:185
  82.3 17.1 %collective-permute-start.4 = (bf16[96,2048]{1,0:T(8,128)(2,1)S(1)}, bf16[96,2048]{1,0:T(8,128)(2,1)S(1)}, u32[]{:S(2)}, u32[]{:S(2)}) collective-permute-start(bf16[96,2048]{1,0:T(8,128)(2,1)S(1)} %get-tuple-element.33), channel_id=1, source_target_pairs={{0,64},{64,128},{128,192},{192,0},{1,65},{65,129},{129,193},{193,1... | collective-permute-start | bytes 1179656 | tf_op jit(solution)/shard_map/ppermute | solution.py:185
  83.5 18.1 %collective-permute-start.5 = (bf16[96,2048]{1,0:T(8,128)(2,1)S(1)}, bf16[96,2048]{1,0:T(8,128)(2,1)S(1)}, u32[]{:S(2)}, u32[]{:S(2)}) collective-permute-start(bf16[96,2048]{1,0:T(8,128)(2,1)S(1)} %get-tuple-element.34), channel_id=1, source_target_pairs={{0,128},{64,192},{128,0},{192,64},{1,129},{65,193},{129,1},{193,65... | collective-permute-start | bytes 1179656 | tf_op jit(solution)/shard_map/ppermute | solution.py:185
  87.1 16.3 %collective-permute-start.6 = (bf16[96,2048]{1,0:T(8,128)(2,1)S(1)}, bf16[96,2048]{1,0:T(8,128)(2,1)S(1)}, u32[]{:S(2)}, u32[]{:S(2)}) collective-permute-start(bf16[96,2048]{1,0:T(8,128)(2,1)S(1)} %get-tuple-element.35), channel_id=1, source_target_pairs={{0,192},{64,0},{128,64},{192,128},{1,193},{65,1},{129,65},{193,129... | collective-permute-start | bytes 1179656 | tf_op jit(solution)/shard_map/ppermute | solution.py:185
  95.9 18.6 %all-to-all-start.2 = ((bf16[8,32,768]{2,1,0:T(8,128)(2,1)}), bf16[8,32,768]{2,1,0:T(8,128)(2,1)S(1)}, u32[]{:S(2)}, u32[]{:S(2)}) async-start(bf16[8,32,768]{2,1,0:T(8,128)(2,1)} %bitcast.15), calls=%async_computation.2 | async-start | bytes 786432 | tf_op jit(solution)/shard_map/all_to_all | solution.py:189
  (3 other events, 2.1 us)
